TPU v7x, 256 devices: a whole 4x4x8 slice. The times are simulated.
256 devices in a mesh: row: 32 (over z_lo, x, core), rhs: 8 (over y, z_hi).
Axes of the slice: x: 4, y: 4, z: 8 (z_hi: 2, z_lo: 4; z = z_hi * 4 + z_lo), core: 2. Of those that a mesh axis runs over, the one named last changes fastest.
Arguments:
- rhs_in: float32 [2, 1024, 16384], P(None, ('rhs', 'row')), may hold values from -6 to 6
- pivots: int32 [16384], replicated, may hold values from 0 to 16383, each once
- owners: int32 [32], replicated, may hold values from 0 to 31, each once
- panel_first: float32 [2, 16384, 512], P(None, 'row'), may hold values from -0.1875 to 0.1875
- panel_second: float32 [2, 16384, 512], P(None, 'row'), may hold values from -0.1875 to 0.1875
- inverse_first: float32 [2, 512, 512], replicated, may hold values from -0.1875 to 0.1875
- inverse_second: float32 [2, 512, 512], replicated, may hold values from -0.1875 to 0.1875
Outputs:
- solved_rhs: float32 [2, 1024, 16384], P(None, 'rhs', 'row')
Inputs may be any that keep to these rules, and one draw needn't show every extreme that they name: `pivots`: each row number occurs once. `owners`: each device index along row occurs once.
All inputs are finite; a program needn't handle non-finite values.
Results may differ from a plain program's by a relative error of at most 0.0001.
Values sent between devices are 32-bit elements; how exact they have to be, the bound alone decides.
No kernel may reach another device: no remote copies, remote signals or barrier semaphores. Data moves between devices by JAX's collectives and lax.ppermute only.
A program may use at most 128 MiB of HBM per device.

v0:
```python
import jax
import jax.numpy as jnp
from jax import lax
from jax.sharding import PartitionSpec as P


def broadcast(shard, axis, root):
    mine = lax.axis_index(axis) == root
    return lax.psum(jnp.where(mine, shard, jnp.zeros_like(shard)), axis)


def complex_product(operand, matrix):
    contract = (((1,), (1,)), ((), ()))

    def multiply(first, second):
        return lax.dot_general(
            first,
            second,
            contract,
            precision=lax.Precision.HIGHEST,
            preferred_element_type=jnp.float32,
        )

    real_part = multiply(operand[0], matrix[0]) - multiply(operand[1], matrix[1])
    imag_part = multiply(operand[0], matrix[1]) + multiply(operand[1], matrix[0])
    return jnp.stack([real_part, imag_part])


def shards(rhs_in, pivots, owners, panel_first, panel_second, inverse_first, inverse_second):
    blocks = owners.shape[0]
    block_size = panel_first.shape[2]
    slot_block = jnp.zeros((blocks,), jnp.int32).at[owners].set(jnp.arange(blocks, dtype=jnp.int32))
    row_index = (
        slot_block[:, None] * block_size + jnp.arange(block_size, dtype=jnp.int32)[None, :]
    ).reshape(-1)
    ordered = jnp.take(rhs_in, jnp.take(pivots, row_index), axis=2)
    my_index = lax.axis_index("row")
    my_block = slot_block[my_index]
    current = lax.all_to_all(ordered, "row", split_axis=2, concat_axis=1, tiled=True)
    sections = ((panel_first, inverse_first), (panel_second, inverse_second))
    for block_step in range(2):
        panel_rows, inverse = sections[block_step]
        holder = owners[block_step]
        solved = complex_product(current, inverse)
        solution = broadcast(solved, "row", holder)
        update = complex_product(solution, panel_rows)
        current = jnp.where(my_block > block_step, current - update, current)
        current = jnp.where(my_block == block_step, solution, current)
    return current


def solution(mesh):
    return jax.shard_map(
        shards,
        mesh=mesh,
        in_specs=(
            P(None, ("rhs", "row"), None),
            P(),
            P(),
            P(None, "row", None),
            P(None, "row", None),
            P(),
            P(),
        ),
        out_specs=P(None, "rhs", "row"),
        check_vma=False,
    )
```

profile of v0, /device:TPU:1, one launch (start us, length us, event | category | flops | bytes accessed | tf_op | source)
XLA Modules:
  0.0 983.9 jit_solution(494485509080680540)
XLA Ops:
  8.2 90.5 %gather_fusion = s32[16384]{0:T(1024)S(1)} fusion(s32[16384]{0:T(1024)S(1)} %copy-done, s32[16384]{0:T(1024)S(1)} %broadcast_clamp_fusion.1), kind=kCustom, calls=%fused_computation | custom fusion | bytes 196608 | tf_op jit(solution)/shard_map/jit(_take)/gather | solution.py:36
  99.0 14.8 %copy.9 = f32[2,4,16384]{1,0,2:T(2,128)} copy(f32[2,4,16384]{2,1,0:T(4,128)S(1)} %copy-done.8) | data formatting | bytes 1048576 | tf_op args[0]
  113.9 118.0 %gather_fusion.1 = f32[16384,2,4]{2,1,0:T(2,128)} fusion(f32[2,4,16384]{1,0,2:T(2,128)} %copy.9, s32[16384]{0:T(1024)S(1)} %broadcast_clamp_fusion), kind=kCustom, calls=%fused_computation.1 | custom fusion | bytes 1114112 | tf_op jit(solution)/shard_map/jit(_take)/gather | solution.py:36
  231.9 59.0 %fusion.56 = f32[16384,2,4]{2,1,0:T(2,128)} fusion(f32[16384,2,4]{2,1,0:T(2,128)} %gather_fusion.1, pred[16384]{0:T(1024)(128)(4,1)S(1)} %compare_and_fusion), kind=kLoop, calls=%fused_computation.89 | loop fusion | flops 131072 | bytes 1064960
  290.9 27.6 %reshape.122 = f32[32,1,4096]{2,1,0:T(1,128)} reshape(f32[16384,2,4]{2,1,0:T(2,128)} %fusion.56) | data formatting | bytes 1048576
  318.5 10.0 %all-to-all-start = ((f32[32,1,4096]{2,1,0:T(1,128)}), f32[32,1,4096]{2,1,0:T(1,128)S(1)}, u32[]{:S(2)}, u32[]{:S(2)}) async-start(f32[32,1,4096]{2,1,0:T(1,128)} %reshape.122), calls=%async_computation | async-start | bytes 1048576 | tf_op jit(solution)/shard_map/all_to_all | solution.py:39
  330.1 14.9 %all-to-all-done = f32[32,1,4096]{2,1,0:T(1,128)S(1)} async-done(((f32[32,1,4096]{2,1,0:T(1,128)}), f32[32,1,4096]{2,1,0:T(1,128)S(1)}, u32[]{:S(2)}, u32[]{:S(2)}) %all-to-all-start) | async-done | bytes 524320 | tf_op jit(solution)/shard_map/all_to_all | solution.py:39
  345.5 1.9 reduce
  347.4 27.8 %reshape.123 = f32[16384,2,4]{2,1,0:T(2,128)} reshape(f32[32,4096]{1,0:T(8,128)S(1)} %reduce) | data formatting | bytes 1048576
  375.2 19.1 %copy.10 = f32[2,4,32,512]{3,1,2,0:T(4,128)S(1)} copy(f32[2,4,32,512]{1,0,3,2:T(2,128)} %bitcast.111) | data formatting | bytes 1048576 | tf_op jit(solution)/shard_map/all_to_all | solution.py:39
  398.6 1.2 fusion.7
  399.8 1.2 fusion.6
  404.7 274.4 %all-reduce.3.cloned.1.call-done = f32[2,128,512]{2,1,0:T(8,128)} async-done(((f32[2,128,512]{2,1,0:T(8,128)}), f32[2,128,512]{2,1,0:T(8,128)}) %all-reduce.3.cloned.1.call-update) | async-done | bytes 524304 | tf_op jit(solution)/shard_map/psum | solution.py:9
  679.1 2.2 fusion.20
  681.3 2.1 fusion.24
  683.4 1.2 fusion.4
  684.6 1.2 fusion.5
  686.2 1.2 fusion.14
  688.5 1.2 fusion.2
  689.7 1.2 fusion.3
  692.9 276.4 %all-reduce.5.cloned.1.call-done = f32[2,128,512]{2,1,0:T(8,128)} async-done(((f32[2,128,512]{2,1,0:T(8,128)}), f32[2,128,512]{2,1,0:T(8,128)}) %all-reduce.5.cloned.1.call-update) | async-done | bytes 524304 | tf_op jit(solution)/shard_map/psum | solution.py:9
  969.4 2.2 fusion.8
  971.6 2.1 fusion.12
  974.9 1.2 fusion.1
  (51 shorter events, 13.9 us)
Async XLA Ops:
  6.5 1.7 copy-start
  8.2 90.8 %copy-start.8 = (f32[2,4,16384]{2,1,0:T(4,128)S(1)}, f32[2,4,16384]{2,1,0:T(4,128)}, u32[]{:S(2)}) copy-start(f32[2,4,16384]{2,1,0:T(4,128)} %param.7) | copy-start | bytes 1572868
  290.9 37.9 %copy-start.9 = (s32[32]{0:T(128)S(1)}, s32[32]{0:T(128)}, u32[]{:S(2)}) copy-start(s32[32]{0:T(128)} %param.9) | copy-start | bytes 388
  318.5 26.4 %all-to-all-start = ((f32[32,1,4096]{2,1,0:T(1,128)}), f32[32,1,4096]{2,1,0:T(1,128)S(1)}, u32[]{:S(2)}, u32[]{:S(2)}) async-start(f32[32,1,4096]{2,1,0:T(1,128)} %reshape.122), calls=%async_computation | async-start | bytes 1048576 | tf_op jit(solution)/shard_map/all_to_all | solution.py:39
  328.6 350.5 %all-reduce.3.cloned.1.call-start = ((), (), s32[]{:S(2)}) async-start(), calls=%async_computation.1 | async-start | bytes 1048576 | tf_op jit(solution)/shard_map/psum | solution.py:9
  375.2 20.0 %copy-start.2 = (f32[2,512,512]{2,1,0:T(8,128)S(1)}, f32[2,512,512]{2,1,0:T(8,128)}, u32[]{:S(2)}) copy-start(f32[2,512,512]{2,1,0:T(8,128)} %param.12) | copy-start | bytes 6291460
  401.0 278.1 %copy-start.3 = (f32[2,512,512]{2,1,0:T(8,128)S(1)}, f32[2,512,512]{2,1,0:T(8,128)}, u32[]{:S(2)}) copy-start(f32[2,512,512]{2,1,0:T(8,128)} %param.10) | copy-start | bytes 6291460
  401.9 567.5 %all-reduce.5.cloned.1.call-start = ((), (), s32[]{:S(2)}) async-start(), calls=%async_computation.2 | async-start | bytes 1048576 | tf_op jit(solution)/shard_map/psum | solution.py:9
  679.1 4.3 copy-start.6
  684.6 1.6 copy-start.4
  689.7 279.7 %copy-start.5 = (f32[2,512,512]{2,1,0:T(8,128)S(1)}, f32[2,512,512]{2,1,0:T(8,128)}, u32[]{:S(2)}) copy-start(f32[2,512,512]{2,1,0:T(8,128)} %param.11) | copy-start | bytes 6291460
  969.4 4.3 copy-start.7
  973.7 3.3 copy-start.1
Sparse Core Ops, SparseCore 0:
  402.0 277.0 all-reduce.2
  691.9 277.4 all-reduce.4
where the time goes:
time: 985 us; the launch traced here: 984 us
  waiting for transfers between devices  566 us (57%)
  local copies, waits for them, and re-layouts  303 us (31%)
  other arithmetic  64.8 us (7%)
  matrix products  22.7 us (2%)
  between operations  17.3 us (2%)
  starting transfers between devices  10.5 us (1%)
    psum x2, waiting for transfers between devices, broadcast(): return lax.psum(jnp.where(mine, shard, jnp.zeros_like(shard)), axis)  551 us
    gather x2, local copies, waits for them, and re-layouts, shards(): ordered = jnp.take(rhs_in, jnp.take(pivots, row_index), axis=2)  209 us
    unnamed x25, local copies, waits for them, and re-layouts  70.7 us
    unnamed x2, other arithmetic  59.1 us
    dot_general x16, matrix products, multiply(): lax.dot_general(first, second, contract, precision=lax.Precision.HIGHEST,...  22.7 us
    all_to_all x3, local copies, waits for them, and re-layouts, shards(): lax.all_to_all(ordered, 'row', split_axis=2, concat_axis=1, tiled=True)  19.8 us
  transfers between devices with their start and end apart: 3, of which 3 were waited for; matrix products, arithmetic and copies ran while one was open for 0% of the time, Pallas kernels for 0%

commit v1 on v0

--- a/solution.py
+++ b/solution.py
@@ -4,9 +4,15 @@
 from jax.sharding import PartitionSpec as P
 
 
+def summed_here(block, name):
+    parts = lax.all_gather(block, name, axis=0, tiled=False)
+    total = parts.sum(axis=0)
+    return total
+
+
 def broadcast(shard, axis, root):
     mine = lax.axis_index(axis) == root
-    return lax.psum(jnp.where(mine, shard, jnp.zeros_like(shard)), axis)
+    return summed_here(jnp.where(mine, shard, jnp.zeros_like(shard)), axis)
 
 
 def complex_product(operand, matrix):

time: 985 us -> 640 us (0.65)
  waiting for transfers between devices: 566 us -> 210 us
  other arithmetic: 64.8 us -> 80.2 us
    psum x2 -> x0, waiting for transfers between devices: 551 us -> none  [broadcast(): return lax.psum(jnp.where(mine, shard, jnp.zeros_like(shard)), axis)]
    all_gather x0 -> x2, waiting for transfers between devices: none -> 195 us  [summed_here(): parts = lax.all_gather(block, name, axis=0, tiled=False)]
    reduce_sum x0 -> x2, other arithmetic: none -> 15.5 us  [summed_here(): total = parts.sum(axis=0)]
    unnamed x25 -> x23, local copies, waits for them, and re-layouts: 70.7 us -> 70.7 us
where the time goes in v1:
time: 640 us
  local copies, waits for them, and re-layouts  303 us (47%)
  waiting for transfers between devices  210 us (33%)
  other arithmetic  80.2 us (13%)
  matrix products  19.1 us (3%)
  between operations  17.3 us (3%)
  starting transfers between devices  10.5 us (2%)
    gather x2, local copies, waits for them, and re-layouts, shards(): ordered = jnp.take(rhs_in, jnp.take(pivots, row_index), axis=2)  208 us
    all_gather x2, waiting for transfers between devices, summed_here(): parts = lax.all_gather(block, name, axis=0, tiled=False)  195 us
    unnamed x23, local copies, waits for them, and re-layouts  70.7 us
    unnamed x2, other arithmetic  59.1 us
    all_to_all x3, local copies, waits for them, and re-layouts, shards(): lax.all_to_all(ordered, 'row', split_axis=2, concat_axis=1, tiled=True)  20.6 us
    dot_general x16, matrix products, multiply(): lax.dot_general(first, second, contract, precision=lax.Precision.HIGHEST,...  19.1 us
    reduce_sum x2, other arithmetic, summed_here(): total = parts.sum(axis=0)  15.5 us
    all_to_all x1, waiting for transfers between devices, shards(): lax.all_to_all(ordered, 'row', split_axis=2, concat_axis=1, tiled=True)  15 us
  transfers between devices with their start and end apart: 3, of which 3 were waited for; matrix products, arithmetic and copies ran while one was open for 0% of the time, Pallas kernels for 0%

profile of v1, /device:TPU:1, one launch (start us, length us, event | category | flops | bytes accessed | tf_op | source)
XLA Modules:
  0.0 639.6 jit_solution(5274886086589267824)
XLA Ops:
  8.2 90.5 %gather_fusion = s32[16384]{0:T(1024)S(1)} fusion(s32[16384]{0:T(1024)S(1)} %copy-done, s32[16384]{0:T(1024)S(1)} %broadcast_clamp_fusion.1), kind=kCustom, calls=%fused_computation | custom fusion | bytes 196608 | tf_op jit(solution)/shard_map/jit(_take)/gather | solution.py:42
  99.0 14.9 %copy.11 = f32[2,4,16384]{1,0,2:T(2,128)} copy(f32[2,4,16384]{2,1,0:T(4,128)S(1)} %copy-done.7) | data formatting | bytes 1048576 | tf_op args[0]
  113.9 117.4 %gather_fusion.1 = f32[16384,2,4]{2,1,0:T(2,128)} fusion(f32[2,4,16384]{1,0,2:T(2,128)} %copy.11, s32[16384]{0:T(1024)S(1)} %broadcast_clamp_fusion), kind=kCustom, calls=%fused_computation.1 | custom fusion | bytes 1114112 | tf_op jit(solution)/shard_map/jit(_take)/gather | solution.py:42
  231.3 59.0 %fusion.56 = f32[16384,2,4]{2,1,0:T(2,128)} fusion(f32[16384,2,4]{2,1,0:T(2,128)} %gather_fusion.1, pred[16384]{0:T(1024)(128)(4,1)S(1)} %compare_and_fusion), kind=kLoop, calls=%fused_computation.89 | loop fusion | flops 131072 | bytes 1064960
  290.3 27.6 %reshape.184 = f32[32,1,4096]{2,1,0:T(1,128)} reshape(f32[16384,2,4]{2,1,0:T(2,128)} %fusion.56) | data formatting | bytes 1048576
  317.9 10.0 %all-to-all-start = ((f32[32,1,4096]{2,1,0:T(1,128)}), f32[32,1,4096]{2,1,0:T(1,128)S(1)}, u32[]{:S(2)}, u32[]{:S(2)}) async-start(f32[32,1,4096]{2,1,0:T(1,128)} %reshape.184), calls=%async_computation | async-start | bytes 1048576 | tf_op jit(solution)/shard_map/all_to_all | solution.py:45
  329.4 15.0 %all-to-all-done = f32[32,1,4096]{2,1,0:T(1,128)S(1)} async-done(((f32[32,1,4096]{2,1,0:T(1,128)}), f32[32,1,4096]{2,1,0:T(1,128)S(1)}, u32[]{:S(2)}, u32[]{:S(2)}) %all-to-all-start) | async-done | bytes 524320 | tf_op jit(solution)/shard_map/all_to_all | solution.py:45
  344.9 1.9 reduce
  346.8 27.8 %reshape.185 = f32[16384,2,4]{2,1,0:T(2,128)} reshape(f32[32,4096]{1,0:T(8,128)S(1)} %reduce) | data formatting | bytes 1048576
  374.6 19.1 %copy.12 = f32[2,4,32,512]{3,1,2,0:T(4,128)S(1)} copy(f32[2,4,32,512]{1,0,3,2:T(2,128)} %bitcast.111) | data formatting | bytes 1048576 | tf_op jit(solution)/shard_map/all_to_all | solution.py:45
  394.6 1.2 fusion.26
  398.0 1.2 fusion.7
  399.2 1.2 fusion.6
  404.9 95.0 %all-gather.3.cloned.1.call-done = f32[32,2,128,512]{3,2,1,0:T(8,128)} async-done(((f32[1,2,128,512]{3,2,1,0:T(8,128)}), f32[32,2,128,512]{3,2,1,0:T(8,128)}) %all-gather.3.cloned.1.call-update) | async-done | bytes 16777232 | tf_op jit(solution)/shard_map/all_gather | solution.py:8
  499.9 7.8 %reduce_sum.18 = f32[2,128,512]{2,1,0:T(8,128)S(1)} reduce(f32[32,2,128,512]{3,2,1,0:T(8,128)} %all-gather.3.cloned.1.call-done, f32[]{:T(128)} %constant.51.clone.1), dimensions={0}, to_apply=%region_1.2 | reduce | flops 4063232 | bytes 17301508 | tf_op jit(solution)/shard_map/reduce_sum | solution.py:9
  510.0 1.2 fusion.4
  515.2 1.2 fusion.2
  516.3 1.2 fusion.3
  519.5 99.5 %all-gather.5.cloned.1.call-done = f32[32,2,128,512]{3,2,1,0:T(8,128)} async-done(((f32[1,2,128,512]{3,2,1,0:T(8,128)}), f32[32,2,128,512]{3,2,1,0:T(8,128)}) %all-gather.5.cloned.1.call-update) | async-done | bytes 16777232 | tf_op jit(solution)/shard_map/all_gather | solution.py:8
  619.1 7.8 %reduce_sum.19 = f32[2,128,512]{2,1,0:T(8,128)S(1)} reduce(f32[32,2,128,512]{3,2,1,0:T(8,128)} %all-gather.5.cloned.1.call-done, f32[]{:T(128)} %constant.51.clone.1), dimensions={0}, to_apply=%region_2.3 | reduce | flops 4063232 | bytes 17301508 | tf_op jit(solution)/shard_map/reduce_sum | solution.py:9
  626.8 1.4 fusion.8
  628.3 1.2 fusion.12
  629.5 1.2 fusion
  630.6 1.2 fusion.1
  (51 shorter events, 17.0 us)
Async XLA Ops:
  6.5 1.7 copy-start
  8.2 90.8 %copy-start.7 = (f32[2,4,16384]{2,1,0:T(4,128)S(1)}, f32[2,4,16384]{2,1,0:T(4,128)}, u32[]{:S(2)}) copy-start(f32[2,4,16384]{2,1,0:T(4,128)} %param.7) | copy-start | bytes 1572868
  290.3 37.9 %copy-start.8 = (s32[32]{0:T(128)S(1)}, s32[32]{0:T(128)}, u32[]{:S(2)}) copy-start(s32[32]{0:T(128)} %param.9) | copy-start | bytes 388
  317.9 26.4 %all-to-all-start = ((f32[32,1,4096]{2,1,0:T(1,128)}), f32[32,1,4096]{2,1,0:T(1,128)S(1)}, u32[]{:S(2)}, u32[]{:S(2)}) async-start(f32[32,1,4096]{2,1,0:T(1,128)} %reshape.184), calls=%async_computation | async-start | bytes 1048576 | tf_op jit(solution)/shard_map/all_to_all | solution.py:45
  328.0 171.9 %all-gather.3.cloned.1.call-start = ((), (), s32[]{:S(2)}) async-start(), calls=%async_computation.1 | async-start | bytes 17301504 | tf_op jit(solution)/shard_map/all_gather | solution.py:8
  374.6 20.0 %copy-start.2 = (f32[2,512,512]{2,1,0:T(8,128)S(1)}, f32[2,512,512]{2,1,0:T(8,128)}, u32[]{:S(2)}) copy-start(f32[2,512,512]{2,1,0:T(8,128)} %param.12) | copy-start | bytes 6291460
  401.3 217.8 %all-gather.5.cloned.1.call-start = ((), (), s32[]{:S(2)}) async-start(), calls=%async_computation.2 | async-start | bytes 17301504 | tf_op jit(solution)/shard_map/all_gather | solution.py:8
  404.9 102.7 %copy-start.3 = (f32[2,512,512]{2,1,0:T(8,128)S(1)}, f32[2,512,512]{2,1,0:T(8,128)}, u32[]{:S(2)}) copy-start(f32[2,512,512]{2,1,0:T(8,128)} %param.10) | copy-start | bytes 6291460
  510.0 2.4 copy-start.6
  511.2 1.6 copy-start.4
  519.5 107.3 %copy-start.5 = (f32[2,512,512]{2,1,0:T(8,128)S(1)}, f32[2,512,512]{2,1,0:T(8,128)}, u32[]{:S(2)}) copy-start(f32[2,512,512]{2,1,0:T(8,128)} %param.11) | copy-start | bytes 6291460
  629.4 3.3 copy-start.1
Sparse Core Ops, SparseCore 0:
  401.4 98.4 all-gather.2
  518.5 100.5 all-gather.4
